TPU v7x, 32 devices: a whole 2x2x4 slice. The times are simulated.
32 devices in a mesh: batch: 4 (over y, x), dom: 8 (over z, core).
Axes of the slice: x: 2, y: 2, z: 4, core: 2. Of those that a mesh axis runs over, the one named last changes fastest.
Arguments:
- cell_feat: bfloat16 [4, 4096, 256], P('batch', 'dom'), may hold values from -6 to 6
- net_feat: bfloat16 [4, 4096, 256], P('batch', 'dom'), may hold values from -6 to 6
- net_grad: bfloat16 [4, 4096, 256], P('batch', 'dom'), may hold values from -6 to 6
- w_first: bfloat16 [512, 512], replicated, may hold values from -0.25 to 0.25
- w_second: bfloat16 [512, 256], replicated, may hold values from -0.25 to 0.25
- pin_cell: int32 [4, 8, 8, 256], P('batch', 'dom'), may hold values from 0 to 511
- pin_net: int32 [4, 8, 8, 256], P('batch', 'dom'), may hold values from 0 to 511
- pin_count: int32 [4, 8, 8], P('batch', 'dom'), may hold values from 224 to 256, as said below
Outputs:
- cell_out: float32 [4, 4096, 256], P('batch', 'dom')
- net_out: float32 [4, 4096, 256], P('batch', 'dom')
- first_total: float32 [512, 512], replicated
- second_total: float32 [512, 256], replicated
Inputs may be any that keep to these rules, and one draw needn't show every extreme that they name: `pin_count`: every partition sends at most 256 live slots to each owner, and in every design each partition fills its slots to some owner.
All inputs are finite; a program needn't handle non-finite values.
Results may differ from a plain program's by a relative error of at most 0.004.
Values may be sent and summed in bfloat16 or wider, within the bound.
A program may use at most 64 MiB of HBM per device.

v0:
```python
import math

import jax
import jax.numpy as jnp
from jax import lax
from jax.sharding import PartitionSpec as P


def backward_core(pin_input, pin_grad, w_first, w_second):
    pre_act = jnp.dot(pin_input, w_first, preferred_element_type=jnp.float32)
    hidden = jax.nn.silu(pre_act).astype(jnp.bfloat16)
    second_part = lax.dot_general(
        hidden, pin_grad, (((0,), (0,)), ((), ())), preferred_element_type=jnp.float32
    )
    hidden_grad = lax.dot_general(
        pin_grad, w_second, (((1,), (1,)), ((), ())), preferred_element_type=jnp.float32
    )
    gate_sig = jax.nn.sigmoid(pre_act)
    pre_grad = (hidden_grad * gate_sig * (1.0 + pre_act * (1.0 - gate_sig))).astype(jnp.bfloat16)
    first_part = lax.dot_general(
        pin_input, pre_grad, (((0,), (0,)), ((), ())), preferred_element_type=jnp.float32
    )
    input_grad = lax.dot_general(
        pre_grad, w_first, (((1,), (1,)), ((), ())), preferred_element_type=jnp.float32
    ).astype(jnp.bfloat16)
    return (input_grad, first_part, second_part)


def segment_rows(row_index, values, segment_count):
    one_hot = (row_index[:, None] == lax.broadcasted_iota(jnp.int32, (1, segment_count), 1)).astype(
        jnp.bfloat16
    )
    return lax.dot_general(
        one_hot, values, (((0,), (0,)), ((), ())), preferred_element_type=jnp.float32
    )


def on_device(cell_feat, net_feat, net_grad, w_first, w_second, pin_cell, pin_net, pin_count):
    owners = lax.axis_size("dom")
    cell_table = cell_feat[0]
    net_table = net_feat[0]
    grad_table = net_grad[0]
    slot_cell = pin_cell[0, 0]
    slot_net = pin_net[0, 0]
    counts = pin_count[0, 0]
    capacity = slot_cell.shape[1]
    feat_width = cell_table.shape[1]
    is_live = lax.broadcasted_iota(jnp.int32, (owners, capacity), 1) < counts[:, None]
    net_code = jnp.where(is_live, slot_net, -1)
    cell_flat = slot_cell.reshape(-1)
    cell_rows = jnp.take(cell_table, cell_flat, axis=0)
    zero_bf = jnp.zeros((), jnp.bfloat16)
    requested = lax.all_to_all(net_code, "dom", split_axis=0, concat_axis=0, tiled=True)
    code_flat = requested.reshape(-1)
    net_index = jnp.maximum(code_flat, 0)
    net_rows = jnp.take(net_table, net_index, axis=0)
    grad_rows = jnp.where(
        (code_flat >= 0)[:, None], jnp.take(grad_table, net_index, axis=0), zero_bf
    )
    got_rows, got_grads = (
        lax.all_to_all(
            net_rows.reshape(owners, capacity, feat_width),
            "dom",
            split_axis=0,
            concat_axis=0,
            tiled=True,
        ),
        lax.all_to_all(
            grad_rows.reshape(owners, capacity, feat_width),
            "dom",
            split_axis=0,
            concat_axis=0,
            tiled=True,
        ),
    )
    pin_input = jnp.concatenate([cell_rows, got_rows.reshape(-1, feat_width)], axis=1)
    input_grad, first_part, second_part = backward_core(
        pin_input, got_grads.reshape(-1, feat_width), w_first, w_second
    )
    cell_out = segment_rows(cell_flat, input_grad[:, :feat_width], cell_table.shape[0])
    returned = lax.all_to_all(
        input_grad[:, feat_width:].reshape(owners, capacity, feat_width),
        "dom",
        split_axis=0,
        concat_axis=0,
        tiled=True,
    )
    net_out = segment_rows(net_index, returned.reshape(-1, feat_width), net_table.shape[0])
    first_sum, second_sum = lax.psum((first_part, second_part), ("batch", "dom"))
    wgrad_scale = 1.0 / math.sqrt(lax.axis_size("batch") * owners * owners * capacity)
    return (cell_out[None], net_out[None], first_sum * wgrad_scale, second_sum * wgrad_scale)


def solution(mesh):
    return jax.shard_map(
        on_device,
        mesh=mesh,
        in_specs=(
            P("batch", "dom", None),
            P("batch", "dom", None),
            P("batch", "dom", None),
            P(),
            P(),
            P("batch", "dom", None, None),
            P("batch", "dom", None, None),
            P("batch", "dom", None),
        ),
        out_specs=(P("batch", "dom", None), P("batch", "dom", None), P(), P()),
        check_vma=False,
    )
```

profile of v0, /device:TPU:0, one launch (start us, length us, event | category | flops | bytes accessed | tf_op | source)
XLA Modules:
  0.0 270.1 jit_solution(1571650209187003646)
XLA Ops:
  7.2 0.0 copy-start
  7.2 0.8 compare_select_fusion
  8.0 11.7 %all_to_all.21 = s32[8,1,256]{2,1,0:T(1,128)S(1)} all-to-all(s32[8,1,256]{2,1,0:T(1,128)S(1)} %compare_select_fusion), channel_id=1, replica_groups=mesh['batch'=4,'dom'=8] {'dom'}, dimensions={0} | all-to-all | bytes 16384 | tf_op jit(solution)/shard_map/all_to_all | solution.py:53
  19.8 0.0 copy-start.1
  19.9 7.7 %gather_fusion.2 = bf16[2048,256]{1,0:T(8,128)(2,1)S(1)} fusion(bf16[512,256]{1,0:T(8,128)(2,1)} %bitcast.26, s32[2048]{0:T(1024)S(1)} %fusion.10), kind=kCustom, calls=%fused_computation.2.clone | custom fusion | bytes 2105344 | tf_op jit(solution)/shard_map/jit(_take)/gather | solution.py:56
  27.5 0.0 copy-done.1
  27.5 7.5 %gather_fusion = bf16[2048,256]{1,0:T(8,128)(2,1)S(1)} fusion(bf16[512,256]{1,0:T(8,128)(2,1)S(1)} %bitcast.27, s32[2048]{0:T(1024)S(1)} %fusion.10), kind=kCustom, calls=%fused_computation.clone | custom fusion | bytes 2105344 | tf_op jit(solution)/shard_map/jit(_take)/gather | solution.py:58
  35.0 0.0 copy-start.4
  35.1 0.0 copy-start.2
  35.1 2.4 select_select_fusion
  37.5 29.7 %all_to_all.22 = bf16[8,256,256]{2,1,0:T(8,128)(2,1)} all-to-all(bf16[8,256,256]{2,1,0:T(8,128)(2,1)S(1)} %bitcast.29), channel_id=1, replica_groups=mesh['batch'=4,'dom'=8] {'dom'}, dimensions={0} | all-to-all | bytes 2097152 | tf_op jit(solution)/shard_map/all_to_all | solution.py:61
  67.2 4.2 %all-to-all-start.1 = ((bf16[8,256,256]{2,1,0:T(8,128)(2,1)}), bf16[8,256,256]{2,1,0:T(8,128)(2,1)}, u32[]{:S(2)}, u32[]{:S(2)}) async-start(bf16[8,256,256]{2,1,0:T(8,128)(2,1)} %bitcast.3), calls=%async_computation.1 | async-start | bytes 2097152 | tf_op jit(solution)/shard_map/all_to_all | solution.py:68
  71.5 0.0 copy-done.4
  71.5 0.0 copy-done.2
  71.5 7.5 %gather_fusion.1 = bf16[2048,256]{1,0:T(8,128)(2,1)S(1)} fusion(bf16[512,256]{1,0:T(8,128)(2,1)S(1)} %bitcast.28, s32[2048]{0:T(1024)S(1)} %fusion.11), kind=kCustom, calls=%fused_computation.1.clone | custom fusion | bytes 2105344 | tf_op jit(solution)/shard_map/jit(_take)/gather | solution.py:51
  79.0 0.4 broadcast_select_fusion
  79.5 0.0 copy-done
  79.5 0.0 copy-start.5
  79.5 4.5 %fusion.6 = f32[2048,512]{1,0:T(8,128)} fusion(bf16[512,512]{1,0:T(8,128)(2,1)S(1)} %copy-done, bf16[2048,256]{1,0:T(8,128)(2,1)} %bitcast.31, bf16[2048,256]{1,0:T(8,128)(2,1)S(1)} %broadcast_select_fusion), kind=kOutput, calls=%fused_computation.16 | convolution fusion | flops 1077936128 | bytes 6815744 | tf_op jit(solution)/shard_map/dot_general | solution.py:10
  84.0 14.1 %all-to-all-done.1 = bf16[8,256,256]{2,1,0:T(8,128)(2,1)} async-done(((bf16[8,256,256]{2,1,0:T(8,128)(2,1)}), bf16[8,256,256]{2,1,0:T(8,128)(2,1)}, u32[]{:S(2)}, u32[]{:S(2)}) %all-to-all-start.1) | async-done | bytes 1048608 | tf_op jit(solution)/shard_map/all_to_all | solution.py:68
  98.1 0.0 copy-done.5
  98.1 4.2 %multiply_convert_fusion.1 = bf16[2048,512]{1,0:T(8,128)(2,1)S(1)} fusion(f32[2048,512]{1,0:T(8,128)} %fusion.6, bf16[2048,256]{1,0:T(8,128)(2,1)} %bitcast.4, bf16[512,256]{1,0:T(8,128)(2,1)S(1)} %copy-done.5), kind=kOutput, calls=%fused_computation.5 | convolution fusion | flops 546308096 | bytes 7602176 | tf_op jit(solution)/shard_map/dot_general | solution.py:15
  102.3 0.0 copy-start.6
  102.3 2.6 convolution_convert_fusion
  104.9 0.0 copy-done.6
  104.9 2.3 slice.15
  107.3 3.6 %all-to-all-start.3 = ((bf16[8,256,256]{2,1,0:T(8,128)(2,1)}), bf16[8,256,256]{2,1,0:T(8,128)(2,1)S(1)}, u32[]{:S(2)}, u32[]{:S(2)}) async-start(bf16[8,256,256]{2,1,0:T(8,128)(2,1)} %bitcast.10), calls=%async_computation.3 | async-start | bytes 2097152 | tf_op jit(solution)/shard_map/all_to_all | solution.py:81
  110.8 0.2 all-reduce.3.cloned.1.call-start
  111.1 0.0 copy-start.3
  111.1 0.0 copy-start.7
  111.1 4.7 %fusion.4 = f32[512,256]{1,0:T(8,128)} fusion(bf16[2048,256]{1,0:T(8,128)(2,1)} %bitcast.4, f32[2048,512]{1,0:T(8,128)} %fusion.6), kind=kOutput, calls=%fused_computation.14 | convolution fusion | flops 542113792 | bytes 5767168 | tf_op jit(solution)/shard_map/dot_general | solution.py:12
  115.8 0.0 copy-done.3
  115.8 0.0 copy-done.7
  115.8 2.2 fusion.5
  118.0 0.0 all-reduce.3.cloned.1.call-update
  118.1 3.6 %fusion.8 = f32[1,512,256]{2,1,0:T(8,128)} fusion(s32[2048]{0:T(1024)S(1)} %bitcast.38, bf16[2048,512]{1,0:T(8,128)(2,1)} %convolution_convert_fusion), kind=kOutput, calls=%fused_computation.18 | convolution fusion | flops 537919488 | bytes 1581056 | tf_op jit(solution)/shard_map/dot_general | solution.py:33
  121.7 135.0 %all-reduce.3.cloned.1.call-done = (f32[512,512]{1,0:T(8,128)}, f32[512,256]{1,0:T(8,128)}) async-done(((f32[512,512]{1,0:T(8,128)}, f32[512,256]{1,0:T(8,128)}), (f32[512,512]{1,0:T(8,128)}, f32[512,256]{1,0:T(8,128)})) %all-reduce.3.cloned.1.call-update) | async-done | bytes 1572880 | tf_op jit(solution)/shard_map/psum | solution.py:89
  256.7 1.9 broadcast_multiply_fusion.1
  258.6 2.3 broadcast_multiply_fusion
  260.9 0.0 all-to-all-done.3
  260.9 2.4 fusion.7
  (8 shorter events, 0.1 us)
Async XLA Ops:
  7.2 72.3 %copy-start = (bf16[512,512]{1,0:T(8,128)(2,1)S(1)}, bf16[512,512]{1,0:T(8,128)(2,1)}, u32[]{:S(2)}) copy-start(bf16[512,512]{1,0:T(8,128)(2,1)} %param.13) | copy-start | bytes 1572868
  19.8 7.7 %copy-start.1 = (bf16[1,512,256]{2,1,0:T(8,128)(2,1)S(1)}, bf16[1,512,256]{2,1,0:T(8,128)(2,1)}, u32[]{:S(2)}) copy-start(bf16[1,512,256]{2,1,0:T(8,128)(2,1)} %param.12) | copy-start | bytes 786436
  35.0 36.4 %copy-start.4 = (s32[1,1,8,256]{3,2,1,0:T(8,128)S(1)}, s32[1,1,8,256]{3,2,1,0:T(8,128)}, u32[]{:S(2)}) copy-start(s32[1,1,8,256]{3,2,1,0:T(8,128)} %param.15) | copy-start | bytes 24580
  35.1 36.4 %copy-start.2 = (bf16[1,512,256]{2,1,0:T(8,128)(2,1)S(1)}, bf16[1,512,256]{2,1,0:T(8,128)(2,1)}, u32[]{:S(2)}) copy-start(bf16[1,512,256]{2,1,0:T(8,128)(2,1)} %param.10) | copy-start | bytes 786436
  67.2 30.8 %all-to-all-start.1 = ((bf16[8,256,256]{2,1,0:T(8,128)(2,1)}), bf16[8,256,256]{2,1,0:T(8,128)(2,1)}, u32[]{:S(2)}, u32[]{:S(2)}) async-start(bf16[8,256,256]{2,1,0:T(8,128)(2,1)} %bitcast.3), calls=%async_computation.1 | async-start | bytes 2097152 | tf_op jit(solution)/shard_map/all_to_all | solution.py:68
  79.5 18.6 %copy-start.5 = (bf16[512,256]{1,0:T(8,128)(2,1)S(1)}, bf16[512,256]{1,0:T(8,128)(2,1)}, u32[]{:S(2)}) copy-start(bf16[512,256]{1,0:T(8,128)(2,1)} %param.14) | copy-start | bytes 786436
  102.3 2.6 copy-start.6
  107.3 153.6 %all-to-all-start.3 = ((bf16[8,256,256]{2,1,0:T(8,128)(2,1)}), bf16[8,256,256]{2,1,0:T(8,128)(2,1)S(1)}, u32[]{:S(2)}, u32[]{:S(2)}) async-start(bf16[8,256,256]{2,1,0:T(8,128)(2,1)} %bitcast.10), calls=%async_computation.3 | async-start | bytes 2097152 | tf_op jit(solution)/shard_map/all_to_all | solution.py:81
  110.8 145.9 %all-reduce.3.cloned.1.call-start = ((), (), s32[]{:S(2)}) async-start(), calls=%async_computation.4 | async-start | bytes 3145728 | tf_op jit(solution)/shard_map/psum | solution.py:89
  111.1 4.7 %copy-start.3 = (bf16[8,256,256]{2,1,0:T(8,128)(2,1)S(1)}, bf16[8,256,256]{2,1,0:T(8,128)(2,1)}, u32[]{:S(2)}) copy-start(bf16[8,256,256]{2,1,0:T(8,128)(2,1)} %all_to_all.22) | copy-start | bytes 3145732
  111.1 4.7 %copy-start.7 = (bf16[2048,512]{1,0:T(8,128)(2,1)S(1)}, bf16[2048,512]{1,0:T(8,128)(2,1)}, u32[]{:S(2)}) copy-start(bf16[2048,512]{1,0:T(8,128)(2,1)} %copy-done.6) | copy-start | bytes 6291460
Sparse Core Ops, SparseCore 0:
  118.2 138.4 all-reduce.2
where the time goes:
time: 271 us; the launch traced here: 270 us
  waiting for transfers between devices  149 us (55%)
  blocking collectives  41.4 us (15%)
  local copies, waits for them, and re-layouts  25.1 us (9%)
  matrix products  24.3 us (9%)
  between operations  14.2 us (5%)
  starting transfers between devices  8.03 us (3%)
  other arithmetic  7.95 us (3%)
    psum x1, waiting for transfers between devices, on_device(): lax.psum((first_part, second_part), ('batch', 'dom'))  135 us
    all_to_all x1, blocking collectives, on_device(): lax.all_to_all(net_rows.reshape(owners, capacity, feat_width), 'dom', spl...  29.7 us
    all_to_all x1, waiting for transfers between devices, on_device(): lax.all_to_all(grad_rows.reshape(owners, capacity, feat_width), 'dom', sp...  14.1 us
    all_to_all x1, blocking collectives, on_device(): lax.all_to_all(net_code, 'dom', split_axis=0, concat_axis=0, tiled=True)  11.7 us
    gather x1, local copies, waits for them, and re-layouts, on_device(): net_rows = jnp.take(net_table, net_index, axis=0)  7.67 us
    gather x1, local copies, waits for them, and re-layouts, on_device(): jnp.take(grad_table, net_index, axis=0)  7.5 us
    gather x1, local copies, waits for them, and re-layouts, on_device(): cell_rows = jnp.take(cell_table, cell_flat, axis=0)  7.5 us
    dot_general x2, matrix products, segment_rows(): lax.dot_general(one_hot, values, (((0,), (0,)), ((), ())), preferred_elem...  5.99 us
  transfers between devices with their start and end apart: 3, of which 2 were waited for; matrix products, arithmetic and copies ran while one was open for 10% of the time, Pallas kernels for 0%

commit v1 on v0

v1 whole, which is shorter than its diff:
```python
import functools
import math

import jax
import jax.numpy as jnp
from jax import lax
from jax.experimental import pallas as pl
from jax.experimental.pallas import tpu as pltpu
from jax.sharding import PartitionSpec as P

BF = jnp.bfloat16
F32 = jnp.float32
MESH = pl.DeviceIdType.MESH


def mm(a, b):
    return jnp.dot(a, b, preferred_element_type=F32)


def mm_t(a, b):
    return lax.dot_general(a, b, (((1,), (1,)), ((), ())), preferred_element_type=F32)


def one_hot_t(row, count):
    at = lax.broadcasted_iota(jnp.int32, (count, row.shape[1]), 0)
    return jnp.where(at == row, 1.0, 0.0).astype(BF)


def kernel(
    batches, owners, rows_z, scale,
    cell, net, grad, w1, w2, slot_cell, code,
    cell_out, net_out, first_out, second_out,
    cell_t, net_t, w1_t, x_t, total,
    send, recv, code_recv, ret_send, ret_recv,
    core_send, core_recv, part_core, bat_send, bat_recv, part_bat, z_send, z_recv, full,
    send_sem, recv_sem, code_ssem, code_rsem, ret_ssem, ret_rsem,
    core_sem, bat_ssem, bat_rsem, z_ssem, z_rsem, gcore_sem, gbat_ssem, gbat_rsem, gz_ssem, gz_rsem,
):
    bat = lax.axis_index("batch")
    me = lax.axis_index("dom")
    feat = cell.shape[1]
    cells = cell.shape[0]
    nets = net.shape[0]
    mid = w1.shape[1]
    core = lax.rem(me, 2)
    depth = owners // 2
    zat = me // 2
    sibling = me + 1 - 2 * core
    half = total.shape[0] // 2

    barrier = pltpu.get_barrier_semaphore()

    def greet_dom(k, carry):
        pl.semaphore_signal(
            barrier, inc=1, device_id=(bat, lax.rem(me + k, owners)), device_id_type=MESH
        )
        return carry

    def greet_batch(k, carry):
        pl.semaphore_signal(
            barrier, inc=1, device_id=(lax.rem(bat + k, batches), me), device_id_type=MESH
        )
        return carry

    lax.fori_loop(1, owners, greet_dom, 0)
    lax.fori_loop(1, batches, greet_batch, 0)

    cell_t[...] = cell[...].T
    code_recv[me] = code[me]
    recv[me] = mm(cell_t[...], one_hot_t(slot_cell[me, 0:1, :], cells)).astype(BF)

    pl.semaphore_wait(barrier, owners + batches - 2)

    def code_copy(to, frm):
        return pltpu.make_async_remote_copy(
            src_ref=code.at[to], dst_ref=code_recv.at[frm],
            send_sem=code_ssem.at[to], recv_sem=code_rsem.at[frm],
            device_id=(bat, to), device_id_type=MESH,
        )

    def row_copy(to, frm):
        return pltpu.make_async_remote_copy(
            src_ref=send.at[to], dst_ref=recv.at[frm],
            send_sem=send_sem.at[to], recv_sem=recv_sem.at[frm],
            device_id=(bat, to), device_id_type=MESH,
        )

    def ret_copy(to, frm):
        return pltpu.make_async_remote_copy(
            src_ref=ret_send.at[to], dst_ref=ret_recv.at[frm],
            send_sem=ret_ssem.at[to], recv_sem=ret_rsem.at[frm],
            device_id=(bat, to), device_id_type=MESH,
        )

    def send_rows(k, carry):
        to = lax.rem(me + k, owners)
        code_copy(to, me).start()
        send[to] = mm(cell_t[...], one_hot_t(slot_cell[to, 0:1, :], cells)).astype(BF)
        row_copy(to, me).start()
        return carry

    lax.fori_loop(1, owners, send_rows, 0)

    net_t[0:feat, :] = net[...].T
    net_t[feat:, :] = grad[...].T
    w1_t[...] = w1[...].T
    net_out[...] = jnp.zeros_like(net_out)
    total[...] = jnp.zeros_like(total)

    def work(src):
        hot = one_hot_t(code_recv[src, 0:1, :], nets)
        rows = mm(net_t[...], hot).astype(BF)
        x_t[0:feat, :] = recv[src]
        x_t[feat:, :] = rows[0:feat, :]
        pin_grad = rows[feat:, :]
        pre = mm(w1_t[...], x_t[...])
        hidden_grad = mm(w2[...], pin_grad)
        sig = jax.nn.sigmoid(pre)
        hidden = (pre * sig).astype(BF)
        pre_grad = (hidden_grad * sig * (1.0 + pre * (1.0 - sig))).astype(BF)
        total[:, 0:mid] += mm_t(x_t[...], pre_grad)
        total[:, mid:] += mm_t(hidden, pin_grad)
        back = mm(w1[...], pre_grad).astype(BF)
        net_out[...] += mm_t(hot, back[feat:, :])
        return back[0:feat, :]

    ret_recv[me] = work(me)

    def step(k, carry):
        src = lax.rem(me - k + owners, owners)
        code_copy(src, src).wait_recv()
        row_copy(src, src).wait_recv()
        ret_send[src] = work(src)
        ret_copy(src, me).start()
        return carry

    lax.fori_loop(1, owners, step, 0)

    core_send[...] = total[pl.ds(pl.multiple_of((1 - core) * half, half), half), :].astype(BF)
    core_copy = pltpu.make_async_remote_copy(
        src_ref=core_send, dst_ref=core_recv, send_sem=core_sem.at[0], recv_sem=core_sem.at[1],
        device_id=(bat, sibling), device_id_type=MESH,
    )
    core_copy.start()
    core_copy.wait()
    mine = total[pl.ds(pl.multiple_of(core * half, half), half), :] + core_recv[...].astype(F32)
    part_core[...] = mine.reshape(part_core.shape)
    bat_send[...] = mine.astype(BF).reshape(bat_send.shape)

    def bat_copy(to, frm):
        return pltpu.make_async_remote_copy(
            src_ref=bat_send.at[to], dst_ref=bat_recv.at[frm],
            send_sem=bat_ssem.at[to], recv_sem=bat_rsem.at[frm],
            device_id=(to, me), device_id_type=MESH,
        )

    def bat_go(k, carry):
        bat_copy(lax.rem(bat + k, batches), bat).start()
        return carry

    lax.fori_loop(1, batches, bat_go, 0)
    part_bat[...] = part_core[bat]

    def bat_add(k, carry):
        frm = lax.rem(bat - k + batches, batches)
        bat_copy(frm, frm).wait_recv()
        part_bat[...] += bat_recv[frm].astype(F32)
        return carry

    lax.fori_loop(1, batches, bat_add, 0)
    split_z = z_send.shape[0] > 1
    z_send[...] = part_bat[...].astype(BF).reshape(z_send.shape)

    def z_copy(to, frm):
        return pltpu.make_async_remote_copy(
            src_ref=z_send.at[to if split_z else 0], dst_ref=z_recv.at[frm],
            send_sem=z_ssem.at[to], recv_sem=z_rsem.at[frm],
            device_id=(bat, 2 * to + core), device_id_type=MESH,
        )

    def z_go(k, carry):
        z_copy(lax.rem(zat + k, depth), zat).start()
        return carry

    lax.fori_loop(1, depth, z_go, 0)
    z_recv[zat] = z_send[zat if split_z else 0]

    def z_wait(k, carry):
        frm = lax.rem(zat - k + depth, depth)
        z_copy(frm, frm).wait_recv()
        return carry

    lax.fori_loop(1, depth, z_wait, 0)
    summed = z_recv[0].astype(F32)
    for other in range(1, depth):
        summed += z_recv[other].astype(F32)
    summed = summed.astype(BF)

    def gz_copy(to, frm):
        spot = full.at[core, bat, pl.ds(frm * rows_z, rows_z), :]
        return pltpu.make_async_remote_copy(
            src_ref=spot, dst_ref=spot,
            send_sem=gz_ssem.at[to], recv_sem=gz_rsem.at[frm],
            device_id=(bat, 2 * to + core), device_id_type=MESH,
        )

    def gz_go(k, carry):
        gz_copy(lax.rem(zat + k, depth), zat).start()
        return carry

    def gz_wait(k, carry):
        frm = lax.rem(zat - k + depth, depth)
        gz_copy(frm, frm).wait_recv()
        return carry

    if split_z:
        full[core, bat, pl.ds(pl.multiple_of(zat * rows_z, rows_z), rows_z), :] = summed
        lax.fori_loop(1, depth, gz_go, 0)
        lax.fori_loop(1, depth, gz_wait, 0)
    else:
        full[core, bat] = summed

    def gbat_copy(to, frm):
        return pltpu.make_async_remote_copy(
            src_ref=full.at[core, frm], dst_ref=full.at[core, frm],
            send_sem=gbat_ssem.at[to], recv_sem=gbat_rsem.at[frm],
            device_id=(to, me), device_id_type=MESH,
        )

    def gbat_go(k, carry):
        gbat_copy(lax.rem(bat + k, batches), bat).start()
        return carry

    def gbat_wait(k, carry):
        frm = lax.rem(bat - k + batches, batches)
        gbat_copy(frm, frm).wait_recv()
        return carry

    lax.fori_loop(1, batches, gbat_go, 0)

    cell_out[...] = mm_t(one_hot_t(slot_cell[me, 0:1, :], cells), ret_recv[me])

    def gather_back(k, carry):
        frm = lax.rem(me + k, owners)
        ret_copy(frm, frm).wait_recv()
        cell_out[...] += mm_t(one_hot_t(slot_cell[frm, 0:1, :], cells), ret_recv[frm])
        return carry

    lax.fori_loop(1, owners, gather_back, 0)

    lax.fori_loop(1, batches, gbat_wait, 0)

    def gcore_copy(frm):
        return pltpu.make_async_remote_copy(
            src_ref=full.at[frm], dst_ref=full.at[frm],
            send_sem=gcore_sem.at[0], recv_sem=gcore_sem.at[1],
            device_id=(bat, sibling), device_id_type=MESH,
        )

    gcore_copy(core).start()
    gcore_copy(1 - core).wait_recv()
    whole = full[...].reshape(total.shape).astype(F32) * scale
    first_out[...] = whole[:, 0:mid]
    second_out[...] = whole[:, mid:]

    def drain_dom(k, carry):
        to = lax.rem(me + k, owners)
        code_copy(to, me).wait_send()
        row_copy(to, me).wait_send()
        ret_copy(to, me).wait_send()
        return carry

    def drain_batch(k, carry):
        to = lax.rem(bat + k, batches)
        bat_copy(to, bat).wait_send()
        gbat_copy(to, bat).wait_send()
        return carry

    def drain_z(k, carry):
        to = lax.rem(zat + k, depth)
        z_copy(to, zat).wait_send()
        if split_z:
            gz_copy(to, zat).wait_send()
        return carry

    lax.fori_loop(1, owners, drain_dom, 0)
    lax.fori_loop(1, batches, drain_batch, 0)
    lax.fori_loop(1, depth, drain_z, 0)
    gcore_copy(core).wait_send()


def on_device(cell_feat, net_feat, net_grad, w_first, w_second, pin_cell, pin_net, pin_count):
    owners = lax.axis_size("dom")
    batches = lax.axis_size("batch")
    cell, net, grad = cell_feat[0], net_feat[0], net_grad[0]
    capacity = pin_cell.shape[3]
    cells, feat = cell.shape
    nets = net.shape[0]
    fan_in, mid = w_first.shape
    width = mid + feat
    depth = owners // 2
    is_live = lax.broadcasted_iota(jnp.int32, (owners, capacity), 1) < pin_count[0, 0][:, None]
    code = jnp.where(is_live, pin_net[0, 0], -1)
    code = jnp.broadcast_to(code[:, None, :], (owners, 8, capacity))
    slot_cell = jnp.broadcast_to(pin_cell[0, 0][:, None, :], (owners, 8, capacity))
    scale = 1.0 / math.sqrt(batches * owners * owners * capacity)
    half = fan_in // 2
    rows_b = half // batches
    split_z = rows_b // depth >= 16
    rows_z = rows_b // depth if split_z else rows_b
    parts_z = depth if split_z else 1
    dma = pltpu.SemaphoreType.DMA
    vmem = pltpu.VMEM
    cell_out, net_out, first, second = pl.pallas_call(
        functools.partial(kernel, batches, owners, rows_z, scale),
        out_shape=(
            jax.ShapeDtypeStruct((cells, feat), F32),
            jax.ShapeDtypeStruct((nets, feat), F32),
            jax.ShapeDtypeStruct((fan_in, mid), F32),
            jax.ShapeDtypeStruct((mid, feat), F32),
        ),
        in_specs=[pl.BlockSpec(memory_space=pltpu.VMEM)] * 7,
        out_specs=[pl.BlockSpec(memory_space=pltpu.VMEM)] * 4,
        scratch_shapes=[
            vmem((feat, cells), BF),
            vmem((2 * feat, nets), BF),
            vmem((mid, fan_in), BF),
            vmem((fan_in, capacity), BF),
            vmem((fan_in, width), F32),
            vmem((owners, feat, capacity), BF),
            vmem((owners, feat, capacity), BF),
            vmem((owners, 8, capacity), jnp.int32),
            vmem((owners, feat, capacity), BF),
            vmem((owners, feat, capacity), BF),
            vmem((half, width), BF),
            vmem((half, width), BF),
            vmem((batches, rows_b, width), F32),
            vmem((batches, rows_b, width), BF),
            vmem((batches, rows_b, width), BF),
            vmem((rows_b, width), F32),
            vmem((parts_z, rows_z, width), BF),
            vmem((depth, rows_z, width), BF),
            vmem((2, batches, rows_b, width), BF),
            dma((owners,)), dma((owners,)), dma((owners,)), dma((owners,)),
            dma((owners,)), dma((owners,)),
            dma((2,)), dma((batches,)), dma((batches,)), dma((depth,)), dma((depth,)),
            dma((2,)), dma((batches,)), dma((batches,)), dma((depth,)), dma((depth,)),
        ],
        compiler_params=pltpu.CompilerParams(
            collective_id=0, has_side_effects=True, vmem_limit_bytes=48 * 1024 * 1024
        ),
    )(cell, net, grad, w_first, w_second, slot_cell, code)
    return (cell_out[None], net_out[None], first, second)


def solution(mesh):
    return jax.shard_map(
        on_device,
        mesh=mesh,
        in_specs=(
            P("batch", "dom", None),
            P("batch", "dom", None),
            P("batch", "dom", None),
            P(),
            P(),
            P("batch", "dom", None, None),
            P("batch", "dom", None, None),
            P("batch", "dom", None),
        ),
        out_specs=(P("batch", "dom", None), P("batch", "dom", None), P(), P()),
        check_vma=False,
    )
```

time: 271 us -> 80.9 us (0.30)
  waiting for transfers between devices: 149 us -> 0 us
  Pallas kernels: 0 us -> 70 us
  blocking collectives: 41.4 us -> 0 us
  matrix products: 24.3 us -> 0 us
  local copies, waits for them, and re-layouts: 25.1 us -> 9.57 us
  between operations: 14.2 us -> 0.67 us
  starting transfers between devices: 8.03 us -> 0 us
  other arithmetic: 7.95 us -> 0.07 us
    psum x1 -> x0, waiting for transfers between devices: 135 us -> none  [on_device(): lax.psum((first_part, second_part), ('batch', 'dom'))]
    pallas_call x0 -> x1, Pallas kernels: none -> 70 us  [on_device(): pl.pallas_call(functools.partial(kernel, batches, owners, rows_z, scale),...]
    all_to_all x2 -> x0, blocking collectives: 41.4 us -> none  [the longest x1 29.7 us: on_device(): lax.all_to_all(net_rows.reshape(owners, capacity, feat_width), 'dom', spl...]
    dot_general x7 -> x0, matrix products: 24.3 us -> none  [the longest x2 5.99 us: segment_rows(): lax.dot_general(one_hot, values, (((0,), (0,)), ((), ())), preferred_elem...]
    gather x3 -> x0, local copies, waits for them, and re-layouts: 22.7 us -> none  [the longest x1 7.67 us: on_device(): net_rows = jnp.take(net_table, net_index, axis=0)]
    all_to_all x2 -> x0, waiting for transfers between devices: 14.1 us -> none  [the longest x1 14.1 us: on_device(): lax.all_to_all(grad_rows.reshape(owners, capacity, feat_width), 'dom', sp...]
    unnamed x17 -> x20, local copies, waits for them, and re-layouts: 0.05 us -> 9.56 us
    all_to_all x2 -> x0, starting transfers between devices: 7.8 us -> none  [the longest x1 4.25 us: on_device(): lax.all_to_all(grad_rows.reshape(owners, capacity, feat_width), 'dom', sp...]
  transfers between devices with their start and end apart: 3 -> 0, of which waited for: 2 -> 0; matrix products, arithmetic and copies ran while one was open for 10% -> 0% of each run, Pallas kernels for 0% -> 0%
where the time goes in v1:
time: 80.9 us; the launch traced here: 80.3 us
  Pallas kernels  70 us (87%)
  local copies, waits for them, and re-layouts  9.57 us (12%)
    pallas_call x1, Pallas kernels, on_device(): pl.pallas_call(functools.partial(kernel, batches, owners, rows_z, scale),...  70 us
    unnamed x20, local copies, waits for them, and re-layouts  9.56 us

profile of v1, /device:TPU:0, one launch (start us, length us, event | category | flops | bytes accessed | tf_op | source)
XLA Modules:
  0.0 80.3 jit_solution(14275654449112259370)
XLA Ops:
  0.6 0.0 copy-start.6
  0.6 0.0 copy-start.7
  0.7 0.7 copy-done.6
  1.3 0.0 copy-done.7
  1.3 0.1 bitcast_select_fusion
  1.4 0.0 copy-start.5
  1.4 0.7 copy-done.5
  2.1 0.0 copy-start
  2.1 1.0 %copy-done = bf16[512,512]{1,0:T(8,128)(2,1)S(1)} copy-done((bf16[512,512]{1,0:T(8,128)(2,1)S(1)}, bf16[512,512]{1,0:T(8,128)(2,1)}, u32[]{:S(2)}) %copy-start) | copy-done | bytes 524312
  3.1 0.0 copy-start.1
  3.2 0.9 %copy-done.1 = bf16[1,512,256]{2,1,0:T(8,128)(2,1)S(1)} copy-done((bf16[1,512,256]{2,1,0:T(8,128)(2,1)S(1)}, bf16[1,512,256]{2,1,0:T(8,128)(2,1)}, u32[]{:S(2)}) %copy-start.1) | copy-done | bytes 262168
  4.1 0.0 copy-start.2
  4.1 0.9 %copy-done.2 = bf16[1,512,256]{2,1,0:T(8,128)(2,1)S(1)} copy-done((bf16[1,512,256]{2,1,0:T(8,128)(2,1)S(1)}, bf16[1,512,256]{2,1,0:T(8,128)(2,1)}, u32[]{:S(2)}) %copy-start.2) | copy-done | bytes 262168
  5.0 0.0 copy-start.3
  5.1 0.9 %copy-done.3 = bf16[1,512,256]{2,1,0:T(8,128)(2,1)S(1)} copy-done((bf16[1,512,256]{2,1,0:T(8,128)(2,1)S(1)}, bf16[1,512,256]{2,1,0:T(8,128)(2,1)}, u32[]{:S(2)}) %copy-start.3) | copy-done | bytes 262168
  6.0 0.0 copy-start.4
  6.0 0.9 %copy-done.4 = bf16[512,256]{1,0:T(8,128)(2,1)S(1)} copy-done((bf16[512,256]{1,0:T(8,128)(2,1)S(1)}, bf16[512,256]{1,0:T(8,128)(2,1)}, u32[]{:S(2)}) %copy-start.4) | copy-done | bytes 262168
  7.0 70.0 %shard_map.111 = (f32[512,256]{1,0:T(8,128)S(1)}, f32[512,256]{1,0:T(8,128)S(1)}, f32[512,512]{1,0:T(8,128)S(1)}, f32[512,256]{1,0:T(8,128)S(1)}) custom-call(bf16[512,256]{1,0:T(8,128)(2,1)S(1)} %bitcast.11, bf16[512,256]{1,0:T(8,128)(2,1)S(1)} %bitcast.12, bf16[512,256]{1,0:T(8,128)(2,1)S(1)} %bitcast.13, bf16[512,512]{1,0:T(8,128)(2,1)S(1)} %copy-done, ...), custom_call_target="tpu_custom_call" | custom-call | tf_op jit(solution)/shard_map/pallas_call | solution.py:314
  77.0 0.8 copy.16
  77.8 0.8 copy.17
  78.5 1.0 %copy.18 = f32[512,512]{1,0:T(8,128)} copy(f32[512,512]{1,0:T(8,128)S(1)} %get-tuple-element.18) | data formatting | bytes 2097152
  79.5 0.8 copy.19
  (2 shorter events, 0.0 us)
Async XLA Ops:
  0.6 0.7 copy-start.6
  0.6 0.7 copy-start.7
  1.4 0.7 copy-start.5
  2.1 1.0 %copy-start = (bf16[512,512]{1,0:T(8,128)(2,1)S(1)}, bf16[512,512]{1,0:T(8,128)(2,1)}, u32[]{:S(2)}) copy-start(bf16[512,512]{1,0:T(8,128)(2,1)} %w1.1) | copy-start | bytes 1572868
  3.1 0.9 %copy-start.1 = (bf16[1,512,256]{2,1,0:T(8,128)(2,1)S(1)}, bf16[1,512,256]{2,1,0:T(8,128)(2,1)}, u32[]{:S(2)}) copy-start(bf16[1,512,256]{2,1,0:T(8,128)(2,1)} %param.8) | copy-start | bytes 786436
  4.1 0.9 %copy-start.2 = (bf16[1,512,256]{2,1,0:T(8,128)(2,1)S(1)}, bf16[1,512,256]{2,1,0:T(8,128)(2,1)}, u32[]{:S(2)}) copy-start(bf16[1,512,256]{2,1,0:T(8,128)(2,1)} %param.9) | copy-start | bytes 786436
  5.0 0.9 %copy-start.3 = (bf16[1,512,256]{2,1,0:T(8,128)(2,1)S(1)}, bf16[1,512,256]{2,1,0:T(8,128)(2,1)}, u32[]{:S(2)}) copy-start(bf16[1,512,256]{2,1,0:T(8,128)(2,1)} %param.10) | copy-start | bytes 786436
  6.0 0.9 %copy-start.4 = (bf16[512,256]{1,0:T(8,128)(2,1)S(1)}, bf16[512,256]{1,0:T(8,128)(2,1)}, u32[]{:S(2)}) copy-start(bf16[512,256]{1,0:T(8,128)(2,1)} %w2.1) | copy-start | bytes 786436

commit v2 on v1

--- a/solution.py
+++ b/solution.py
@@ -27,12 +27,14 @@
 
 
 def kernel(
-    batches, owners, rows_z, scale,
-    cell, net, grad, w1, w2, slot_cell, code,
-    cell_out, net_out, first_out, second_out,
-    cell_t, net_t, w1_t, x_t, total,
+    batches, owners, rows_z,
+    cell_hbm, net_hbm, grad_hbm, w1_hbm, w2_hbm, cell_pin_hbm, net_pin_hbm, count_hbm,
+    cell_out, net_out, full,
+    cell, net, grad, w1, w2, slot_cell, net_pin, count, code,
+    cell_t, net_t, w1_t, x_t, g_t, hot, total,
     send, recv, code_recv, ret_send, ret_recv,
-    core_send, core_recv, part_core, bat_send, bat_recv, part_bat, z_send, z_recv, full,
+    core_send, core_recv, part_core, bat_send, bat_recv, part_bat, z_send, z_recv,
+    load_sem,
     send_sem, recv_sem, code_ssem, code_rsem, ret_ssem, ret_rsem,
     core_sem, bat_ssem, bat_rsem, z_ssem, z_rsem, gcore_sem, gbat_ssem, gbat_rsem, gz_ssem, gz_rsem,
 ):
@@ -48,6 +50,18 @@
     sibling = me + 1 - 2 * core
     half = total.shape[0] // 2
 
+    loads = [
+        pltpu.make_async_copy(a, b, load_sem.at[i])
+        for i, (a, b) in enumerate(
+            (
+                (cell_hbm, cell), (cell_pin_hbm, slot_cell), (net_pin_hbm, net_pin),
+                (count_hbm, count), (net_hbm, net), (grad_hbm, grad), (w1_hbm, w1), (w2_hbm, w2),
+            )
+        )
+    ]
+    for load in loads:
+        load.start()
+
     barrier = pltpu.get_barrier_semaphore()
 
     def greet_dom(k, carry):
@@ -65,9 +79,22 @@
     lax.fori_loop(1, owners, greet_dom, 0)
     lax.fori_loop(1, batches, greet_batch, 0)
 
+    for load in loads[:4]:
+        load.wait()
     cell_t[...] = cell[...].T
+    cap = code.shape[2]
+    lane = lax.broadcasted_iota(jnp.int32, (8, cap), 1)
+
+    def cell_hot(to):
+        return one_hot_t(slot_cell[pl.ds(to, 1), :], cells)
+
+    def net_code(to, carry):
+        code[to] = jnp.where(lane < count[0, to], net_pin[pl.ds(to, 1), :], -1)
+        return carry
+
+    lax.fori_loop(0, owners, net_code, 0)
     code_recv[me] = code[me]
-    recv[me] = mm(cell_t[...], one_hot_t(slot_cell[me, 0:1, :], cells)).astype(BF)
+    recv[me] = mm(cell_t[...], cell_hot(me)).astype(BF)
 
     pl.semaphore_wait(barrier, owners + batches - 2)
 
@@ -92,49 +119,64 @@
             device_id=(bat, to), device_id_type=MESH,
         )
 
-    def send_rows(k, carry):
-        to = lax.rem(me + k, owners)
+    def send_to(to):
         code_copy(to, me).start()
-        send[to] = mm(cell_t[...], one_hot_t(slot_cell[to, 0:1, :], cells)).astype(BF)
+        send[to] = mm(cell_t[...], cell_hot(to)).astype(BF)
         row_copy(to, me).start()
-        return carry
-
-    lax.fori_loop(1, owners, send_rows, 0)
-
+
+    def send_rows(j, carry):
+        chip = lax.rem(zat - j + depth, depth)
+        for i in range(2):
+            send_to(2 * chip + i)
+        return carry
+
+    send_to(sibling)
+    lax.fori_loop(1, depth, send_rows, 0)
+
+    for load in loads[4:]:
+        load.wait()
     net_t[0:feat, :] = net[...].T
     net_t[feat:, :] = grad[...].T
     w1_t[...] = w1[...].T
     net_out[...] = jnp.zeros_like(net_out)
     total[...] = jnp.zeros_like(total)
 
-    def work(src):
-        hot = one_hot_t(code_recv[src, 0:1, :], nets)
-        rows = mm(net_t[...], hot).astype(BF)
-        x_t[0:feat, :] = recv[src]
+    def step(j, carry):
+        chip = lax.rem(zat + j, depth)
+        for i in range(2):
+            src = 2 * chip + i
+            spot = pl.ds(i * cap, cap)
+
+            @pl.when(src != me)
+            def _():
+                code_copy(src, src).wait_recv()
+                row_copy(src, src).wait_recv()
+
+            hot[:, spot] = one_hot_t(code_recv[src, 0:1, :], nets)
+            x_t[0:feat, spot] = recv[src]
+        rows = mm(net_t[...], hot[...]).astype(BF)
         x_t[feat:, :] = rows[0:feat, :]
-        pin_grad = rows[feat:, :]
+        g_t[...] = rows[feat:, :]
         pre = mm(w1_t[...], x_t[...])
-        hidden_grad = mm(w2[...], pin_grad)
-        sig = jax.nn.sigmoid(pre)
+        hidden_grad = mm(w2[...], g_t[...])
+        sig = 0.5 + 0.5 * jnp.tanh(0.5 * pre)
         hidden = (pre * sig).astype(BF)
         pre_grad = (hidden_grad * sig * (1.0 + pre * (1.0 - sig))).astype(BF)
+        back = mm(w1[...], pre_grad).astype(BF)
+        for i in range(2):
+            src = 2 * chip + i
+            ret_send[src] = back[0:feat, i * cap : (i + 1) * cap]
+
+            @pl.when(src != me)
+            def _():
+                ret_copy(src, me).start()
+
         total[:, 0:mid] += mm_t(x_t[...], pre_grad)
-        total[:, mid:] += mm_t(hidden, pin_grad)
-        back = mm(w1[...], pre_grad).astype(BF)
-        net_out[...] += mm_t(hot, back[feat:, :])
-        return back[0:feat, :]
-
-    ret_recv[me] = work(me)
-
-    def step(k, carry):
-        src = lax.rem(me - k + owners, owners)
-        code_copy(src, src).wait_recv()
-        row_copy(src, src).wait_recv()
-        ret_send[src] = work(src)
-        ret_copy(src, me).start()
-        return carry
-
-    lax.fori_loop(1, owners, step, 0)
+        total[:, mid:] += mm_t(hidden, g_t[...])
+        net_out[...] += mm_t(hot[...], back[feat:, :])
+        return carry
+
+    lax.fori_loop(0, depth, step, 0)
 
     core_send[...] = total[pl.ds(pl.multiple_of((1 - core) * half, half), half), :].astype(BF)
     core_copy = pltpu.make_async_remote_copy(
@@ -238,12 +280,12 @@
 
     lax.fori_loop(1, batches, gbat_go, 0)
 
-    cell_out[...] = mm_t(one_hot_t(slot_cell[me, 0:1, :], cells), ret_recv[me])
+    cell_out[...] = mm_t(cell_hot(me), ret_send[me])
 
     def gather_back(k, carry):
         frm = lax.rem(me + k, owners)
         ret_copy(frm, frm).wait_recv()
-        cell_out[...] += mm_t(one_hot_t(slot_cell[frm, 0:1, :], cells), ret_recv[frm])
+        cell_out[...] += mm_t(cell_hot(frm), ret_recv[frm])
         return carry
 
     lax.fori_loop(1, owners, gather_back, 0)
@@ -259,9 +301,6 @@
 
     gcore_copy(core).start()
     gcore_copy(1 - core).wait_recv()
-    whole = full[...].reshape(total.shape).astype(F32) * scale
-    first_out[...] = whole[:, 0:mid]
-    second_out[...] = whole[:, mid:]
 
     def drain_dom(k, carry):
         to = lax.rem(me + k, owners)
@@ -287,6 +326,33 @@
     lax.fori_loop(1, batches, drain_batch, 0)
     lax.fori_loop(1, depth, drain_z, 0)
     gcore_copy(core).wait_send()
+
+
+def finish(
+    scale, cell_sum, net_sum, full, cell_out, net_out, first_out, second_out,
+    held, first, second, sem,
+):
+    take = pltpu.make_async_copy(full, held, sem.at[4])
+    take.start()
+    copies = [
+        pltpu.make_async_copy(a, b, sem.at[i])
+        for i, (a, b) in enumerate(
+            (
+                (cell_sum, cell_out), (net_sum, net_out),
+                (first, first_out), (second, second_out),
+            )
+        )
+    ]
+    copies[0].start()
+    copies[1].start()
+    mid = first.shape[1]
+    take.wait()
+    first[...] = held[:, 0:mid].astype(F32) * scale
+    copies[2].start()
+    second[...] = held[:, mid:].astype(F32) * scale
+    copies[3].start()
+    for copy in copies:
+        copy.wait()
 
 
 def on_device(cell_feat, net_feat, net_grad, w_first, w_second, pin_cell, pin_net, pin_count):
@@ -299,10 +365,6 @@
     fan_in, mid = w_first.shape
     width = mid + feat
     depth = owners // 2
-    is_live = lax.broadcasted_iota(jnp.int32, (owners, capacity), 1) < pin_count[0, 0][:, None]
-    code = jnp.where(is_live, pin_net[0, 0], -1)
-    code = jnp.broadcast_to(code[:, None, :], (owners, 8, capacity))
-    slot_cell = jnp.broadcast_to(pin_cell[0, 0][:, None, :], (owners, 8, capacity))
     scale = 1.0 / math.sqrt(batches * owners * owners * capacity)
     half = fan_in // 2
     rows_b = half // batches
@@ -311,21 +373,33 @@
     parts_z = depth if split_z else 1
     dma = pltpu.SemaphoreType.DMA
     vmem = pltpu.VMEM
-    cell_out, net_out, first, second = pl.pallas_call(
-        functools.partial(kernel, batches, owners, rows_z, scale),
+    hbm = pl.BlockSpec(memory_space=pltpu.HBM)
+    on_chip = pl.BlockSpec(memory_space=pltpu.VMEM)
+    cell_sum, net_sum, full = pl.pallas_call(
+        functools.partial(kernel, batches, owners, rows_z),
         out_shape=(
             jax.ShapeDtypeStruct((cells, feat), F32),
             jax.ShapeDtypeStruct((nets, feat), F32),
-            jax.ShapeDtypeStruct((fan_in, mid), F32),
-            jax.ShapeDtypeStruct((mid, feat), F32),
+            jax.ShapeDtypeStruct((2, batches, rows_b, width), BF),
         ),
-        in_specs=[pl.BlockSpec(memory_space=pltpu.VMEM)] * 7,
-        out_specs=[pl.BlockSpec(memory_space=pltpu.VMEM)] * 4,
+        in_specs=[hbm] * 8,
+        out_specs=[on_chip] * 3,
         scratch_shapes=[
+            vmem((cells, feat), BF),
+            vmem((nets, feat), BF),
+            vmem((nets, feat), BF),
+            vmem((fan_in, mid), BF),
+            vmem((mid, feat), BF),
+            vmem((owners, capacity), jnp.int32),
+            vmem((owners, capacity), jnp.int32),
+            pltpu.SMEM((1, owners), jnp.int32),
+            vmem((owners, 8, capacity), jnp.int32),
             vmem((feat, cells), BF),
             vmem((2 * feat, nets), BF),
             vmem((mid, fan_in), BF),
-            vmem((fan_in, capacity), BF),
+            vmem((fan_in, 2 * capacity), BF),
+            vmem((feat, 2 * capacity), BF),
+            vmem((nets, 2 * capacity), BF),
             vmem((fan_in, width), F32),
             vmem((owners, feat, capacity), BF),
             vmem((owners, feat, capacity), BF),
@@ -340,16 +414,28 @@
             vmem((rows_b, width), F32),
             vmem((parts_z, rows_z, width), BF),
             vmem((depth, rows_z, width), BF),
-            vmem((2, batches, rows_b, width), BF),
+            dma((8,)),
             dma((owners,)), dma((owners,)), dma((owners,)), dma((owners,)),
             dma((owners,)), dma((owners,)),
             dma((2,)), dma((batches,)), dma((batches,)), dma((depth,)), dma((depth,)),
             dma((2,)), dma((batches,)), dma((batches,)), dma((depth,)), dma((depth,)),
         ],
         compiler_params=pltpu.CompilerParams(
-            collective_id=0, has_side_effects=True, vmem_limit_bytes=48 * 1024 * 1024
+            collective_id=0, has_side_effects=True, vmem_limit_bytes=60 * 1024 * 1024
         ),
-    )(cell, net, grad, w_first, w_second, slot_cell, code)
+    )(cell, net, grad, w_first, w_second, pin_cell[0, 0], pin_net[0, 0], pin_count[0])
+    cell_out, net_out, first, second = pl.pallas_call(
+        functools.partial(finish, scale),
+        out_shape=(
+            jax.ShapeDtypeStruct((cells, feat), F32),
+            jax.ShapeDtypeStruct((nets, feat), F32),
+            jax.ShapeDtypeStruct((fan_in, mid), F32),
+            jax.ShapeDtypeStruct((mid, feat), F32),
+        ),
+        in_specs=[hbm] * 3,
+        out_specs=[hbm] * 4,
+        scratch_shapes=[vmem((fan_in, width), BF), vmem((fan_in, mid), F32), vmem((mid, feat), F32), dma((5,))],
+    )(cell_sum, net_sum, full.reshape(fan_in, width))
     return (cell_out[None], net_out[None], first, second)
 
 

time: 80.9 us -> 107 us (1.32)
  Pallas kernels: 70 us -> 106 us
  local copies, waits for them, and re-layouts: 9.57 us -> 0 us
    pallas_call x1 -> x2, Pallas kernels: 70 us -> 106 us  [the longest x1 73.1 us: on_device(): pl.pallas_call(functools.partial(kernel, batches, owners, rows_z), out_sh...]
    unnamed x20 -> x0, local copies, waits for them, and re-layouts: 9.56 us -> none
where the time goes in v2:
time: 107 us
  Pallas kernels  106 us (99%)
    pallas_call x1, Pallas kernels, on_device(): pl.pallas_call(functools.partial(kernel, batches, owners, rows_z), out_sh...  73.1 us
    pallas_call x1, Pallas kernels, on_device(): pl.pallas_call(functools.partial(finish, scale), out_shape=(jax.ShapeDtyp...  32.9 us

profile of v2, /device:TPU:0, one launch (start us, length us, event | category | flops | bytes accessed | tf_op | source)
XLA Modules:
  0.0 106.6 jit_solution(13418087924902474974)
XLA Ops:
  0.6 73.1 %shard_map.111 = (f32[512,256]{1,0:T(8,128)}, f32[512,256]{1,0:T(8,128)}, bf16[2,4,64,768]{3,2,1,0:T(8,128)(2,1)}) custom-call(bf16[512,256]{1,0:T(8,128)(2,1)} %bitcast.10, bf16[512,256]{1,0:T(8,128)(2,1)} %bitcast.11, bf16[512,256]{1,0:T(8,128)(2,1)} %bitcast.12, bf16[512,512]{1,0:T(8,128)(2,1)} %w1_hbm.1, bf16[512,256]{1,0:T(8,128)(2,1)} %w2_hbm.1, ...), custom_call_target="tpu_custom_call" | custom-call | tf_op jit(solution)/shard_map/pallas_call | solution.py:378
  73.7 32.9 %shard_map.112 = (f32[512,256]{1,0:T(8,128)}, f32[512,256]{1,0:T(8,128)}, f32[512,512]{1,0:T(8,128)}, f32[512,256]{1,0:T(8,128)}) custom-call(f32[512,256]{1,0:T(8,128)} %get-tuple-element.11.cell_sum, f32[512,256]{1,0:T(8,128)} %get-tuple-element.12.net_sum, bf16[512,768]{1,0:T(8,128)(2,1)} %bitcast.9), custom_call_target="tpu_custom_call" | custom-call | tf_op jit(solution)/shard_map/pallas_call | solution.py:427

commit v3 on v2

--- a/solution.py
+++ b/solution.py
@@ -31,7 +31,7 @@
     cell_hbm, net_hbm, grad_hbm, w1_hbm, w2_hbm, cell_pin_hbm, net_pin_hbm, count_hbm,
     cell_out, net_out, full,
     cell, net, grad, w1, w2, slot_cell, net_pin, count, code,
-    cell_t, net_t, w1_t, x_t, g_t, hot, total,
+    cell_t, net_t, w1_t, cell_all, net_all, grad_all, hot_all, pre_all, hid_grad_all, pre_grad_all, total,
     send, recv, code_recv, ret_send, ret_recv,
     core_send, core_recv, part_core, bat_send, bat_recv, part_bat, z_send, z_recv,
     load_sem,
@@ -120,7 +120,6 @@
         )
 
     def send_to(to):
-        code_copy(to, me).start()
         send[to] = mm(cell_t[...], cell_hot(to)).astype(BF)
         row_copy(to, me).start()
 
@@ -130,6 +129,11 @@
             send_to(2 * chip + i)
         return carry
 
+    def send_codes(k, carry):
+        code_copy(lax.rem(me + k, owners), me).start()
+        return carry
+
+    lax.fori_loop(1, owners, send_codes, 0)
     send_to(sibling)
     lax.fori_loop(1, depth, send_rows, 0)
 
@@ -138,45 +142,57 @@
     net_t[0:feat, :] = net[...].T
     net_t[feat:, :] = grad[...].T
     w1_t[...] = w1[...].T
-    net_out[...] = jnp.zeros_like(net_out)
     total[...] = jnp.zeros_like(total)
 
-    def step(j, carry):
+    def early(j, carry):
         chip = lax.rem(zat + j, depth)
         for i in range(2):
             src = 2 * chip + i
-            spot = pl.ds(i * cap, cap)
 
             @pl.when(src != me)
             def _():
                 code_copy(src, src).wait_recv()
+
+            hot_all[j, :, i * cap : (i + 1) * cap] = one_hot_t(code_recv[src, 0:1, :], nets)
+        rows = mm(net_t[...], hot_all[j]).astype(BF)
+        net_all[j] = rows[0:feat, :]
+        grad_all[j] = rows[feat:, :]
+        pre_all[j] = mm(w1_t[:, feat:], net_all[j])
+        hid_grad_all[j] = mm(w2[...], grad_all[j])
+        return carry
+
+    lax.fori_loop(0, depth, early, 0)
+
+    def late(j, carry):
+        chip = lax.rem(zat + j, depth)
+        for i in range(2):
+            src = 2 * chip + i
+
+            @pl.when(src != me)
+            def _():
                 row_copy(src, src).wait_recv()
 
-            hot[:, spot] = one_hot_t(code_recv[src, 0:1, :], nets)
-            x_t[0:feat, spot] = recv[src]
-        rows = mm(net_t[...], hot[...]).astype(BF)
-        x_t[feat:, :] = rows[0:feat, :]
-        g_t[...] = rows[feat:, :]
-        pre = mm(w1_t[...], x_t[...])
-        hidden_grad = mm(w2[...], g_t[...])
+            cell_all[j, :, i * cap : (i + 1) * cap] = recv[src]
+        pre = pre_all[j] + mm(w1_t[:, 0:feat], cell_all[j])
         sig = 0.5 + 0.5 * jnp.tanh(0.5 * pre)
         hidden = (pre * sig).astype(BF)
-        pre_grad = (hidden_grad * sig * (1.0 + pre * (1.0 - sig))).astype(BF)
-        back = mm(w1[...], pre_grad).astype(BF)
+        pre_grad = (hid_grad_all[j] * sig * (1.0 + pre * (1.0 - sig))).astype(BF)
+        pre_grad_all[j] = pre_grad
+        back = mm(w1[0:feat, :], pre_grad).astype(BF)
         for i in range(2):
             src = 2 * chip + i
-            ret_send[src] = back[0:feat, i * cap : (i + 1) * cap]
+            ret_send[src] = back[:, i * cap : (i + 1) * cap]
 
             @pl.when(src != me)
             def _():
                 ret_copy(src, me).start()
 
-        total[:, 0:mid] += mm_t(x_t[...], pre_grad)
-        total[:, mid:] += mm_t(hidden, g_t[...])
-        net_out[...] += mm_t(hot[...], back[feat:, :])
-        return carry
-
-    lax.fori_loop(0, depth, step, 0)
+        total[0:feat, 0:mid] += mm_t(cell_all[j], pre_grad)
+        total[feat:, 0:mid] += mm_t(net_all[j], pre_grad)
+        total[:, mid:] += mm_t(hidden, grad_all[j])
+        return carry
+
+    lax.fori_loop(0, depth, late, 0)
 
     core_send[...] = total[pl.ds(pl.multiple_of((1 - core) * half, half), half), :].astype(BF)
     core_copy = pltpu.make_async_remote_copy(
@@ -184,6 +200,14 @@
         device_id=(bat, sibling), device_id_type=MESH,
     )
     core_copy.start()
+    net_out[...] = jnp.zeros_like(net_out)
+
+    def net_side(j, carry):
+        back = mm(w1[feat:, :], pre_grad_all[j]).astype(BF)
+        net_out[...] += mm_t(hot_all[j], back)
+        return carry
+
+    lax.fori_loop(0, depth, net_side, 0)
     core_copy.wait()
     mine = total[pl.ds(pl.multiple_of(core * half, half), half), :] + core_recv[...].astype(F32)
     part_core[...] = mine.reshape(part_core.shape)
@@ -280,6 +304,17 @@
 
     lax.fori_loop(1, batches, gbat_go, 0)
 
+    lax.fori_loop(1, batches, gbat_wait, 0)
+
+    def gcore_copy(frm):
+        return pltpu.make_async_remote_copy(
+            src_ref=full.at[frm], dst_ref=full.at[frm],
+            send_sem=gcore_sem.at[0], recv_sem=gcore_sem.at[1],
+            device_id=(bat, sibling), device_id_type=MESH,
+        )
+
+    gcore_copy(core).start()
+
     cell_out[...] = mm_t(cell_hot(me), ret_send[me])
 
     def gather_back(k, carry):
@@ -290,16 +325,6 @@
 
     lax.fori_loop(1, owners, gather_back, 0)
 
-    lax.fori_loop(1, batches, gbat_wait, 0)
-
-    def gcore_copy(frm):
-        return pltpu.make_async_remote_copy(
-            src_ref=full.at[frm], dst_ref=full.at[frm],
-            send_sem=gcore_sem.at[0], recv_sem=gcore_sem.at[1],
-            device_id=(bat, sibling), device_id_type=MESH,
-        )
-
-    gcore_copy(core).start()
     gcore_copy(1 - core).wait_recv()
 
     def drain_dom(k, carry):
@@ -328,31 +353,12 @@
     gcore_copy(core).wait_send()
 
 
-def finish(
-    scale, cell_sum, net_sum, full, cell_out, net_out, first_out, second_out,
-    held, first, second, sem,
-):
-    take = pltpu.make_async_copy(full, held, sem.at[4])
-    take.start()
-    copies = [
-        pltpu.make_async_copy(a, b, sem.at[i])
-        for i, (a, b) in enumerate(
-            (
-                (cell_sum, cell_out), (net_sum, net_out),
-                (first, first_out), (second, second_out),
-            )
-        )
-    ]
-    copies[0].start()
-    copies[1].start()
+def finish(scale, cell_sum, net_sum, full, cell_out, net_out, first, second):
     mid = first.shape[1]
-    take.wait()
-    first[...] = held[:, 0:mid].astype(F32) * scale
-    copies[2].start()
-    second[...] = held[:, mid:].astype(F32) * scale
-    copies[3].start()
-    for copy in copies:
-        copy.wait()
+    cell_out[...] = cell_sum[...]
+    net_out[...] = net_sum[...]
+    first[...] = full[:, 0:mid].astype(F32) * scale
+    second[...] = full[:, mid:].astype(F32) * scale
 
 
 def on_device(cell_feat, net_feat, net_grad, w_first, w_second, pin_cell, pin_net, pin_count):
@@ -375,6 +381,10 @@
     vmem = pltpu.VMEM
     hbm = pl.BlockSpec(memory_space=pltpu.HBM)
     on_chip = pl.BlockSpec(memory_space=pltpu.VMEM)
+
+    def block(rows, columns):
+        return pl.BlockSpec((rows // 4, columns), lambda i: (i, 0))
+
     cell_sum, net_sum, full = pl.pallas_call(
         functools.partial(kernel, batches, owners, rows_z),
         out_shape=(
@@ -397,9 +407,13 @@
             vmem((feat, cells), BF),
             vmem((2 * feat, nets), BF),
             vmem((mid, fan_in), BF),
-            vmem((fan_in, 2 * capacity), BF),
-            vmem((feat, 2 * capacity), BF),
-            vmem((nets, 2 * capacity), BF),
+            vmem((depth, feat, 2 * capacity), BF),
+            vmem((depth, feat, 2 * capacity), BF),
+            vmem((depth, feat, 2 * capacity), BF),
+            vmem((depth, nets, 2 * capacity), BF),
+            vmem((depth, mid, 2 * capacity), F32),
+            vmem((depth, mid, 2 * capacity), F32),
+            vmem((depth, mid, 2 * capacity), BF),
             vmem((fan_in, width), F32),
             vmem((owners, feat, capacity), BF),
             vmem((owners, feat, capacity), BF),
@@ -432,9 +446,9 @@
             jax.ShapeDtypeStruct((fan_in, mid), F32),
             jax.ShapeDtypeStruct((mid, feat), F32),
         ),
-        in_specs=[hbm] * 3,
-        out_specs=[hbm] * 4,
-        scratch_shapes=[vmem((fan_in, width), BF), vmem((fan_in, mid), F32), vmem((mid, feat), F32), dma((5,))],
+        grid=(4,),
+        in_specs=[block(cells, feat), block(nets, feat), block(fan_in, width)],
+        out_specs=[block(cells, feat), block(nets, feat), block(fan_in, mid), block(mid, feat)],
     )(cell_sum, net_sum, full.reshape(fan_in, width))
     return (cell_out[None], net_out[None], first, second)
 

time: 107 us -> 77.4 us (0.72)
  Pallas kernels: 106 us -> 76.5 us
    pallas_call x1, Pallas kernels: 32.9 us -> 3.85 us  [on_device(): pl.pallas_call(functools.partial(finish, scale), out_shape=(jax.ShapeDtyp...]
where the time goes in v3:
time: 77.4 us; the launch traced here: 77.2 us
  Pallas kernels  76.5 us (99%)
    pallas_call x1, Pallas kernels, on_device(): pl.pallas_call(functools.partial(kernel, batches, owners, rows_z), out_sh...  72.7 us
    pallas_call x1, Pallas kernels, on_device(): pl.pallas_call(functools.partial(finish, scale), out_shape=(jax.ShapeDtyp...  3.85 us

profile of v3, /device:TPU:0, one launch (start us, length us, event | category | flops | bytes accessed | tf_op | source)
XLA Modules:
  0.0 77.2 jit_solution(9083843838128850700)
XLA Ops:
  0.6 72.7 %shard_map.111 = (f32[512,256]{1,0:T(8,128)}, f32[512,256]{1,0:T(8,128)}, bf16[2,4,64,768]{3,2,1,0:T(8,128)(2,1)}) custom-call(bf16[512,256]{1,0:T(8,128)(2,1)} %bitcast.10, bf16[512,256]{1,0:T(8,128)(2,1)} %bitcast.11, bf16[512,256]{1,0:T(8,128)(2,1)} %bitcast.12, bf16[512,512]{1,0:T(8,128)(2,1)} %w1_hbm.1, bf16[512,256]{1,0:T(8,128)(2,1)} %w2_hbm.1, ...), custom_call_target="tpu_custom_call" | custom-call | tf_op jit(solution)/shard_map/pallas_call | solution.py:388
  73.3 3.8 %shard_map.112 = (f32[512,256]{1,0:T(8,128)}, f32[512,256]{1,0:T(8,128)}, f32[512,512]{1,0:T(8,128)}, f32[512,256]{1,0:T(8,128)}) custom-call(f32[512,256]{1,0:T(8,128)} %get-tuple-element.11.cell_sum, f32[512,256]{1,0:T(8,128)} %get-tuple-element.12.net_sum, bf16[512,768]{1,0:T(8,128)(2,1)} %bitcast.9), custom_call_target="tpu_custom_call" | custom-call | tf_op jit(solution)/shard_map/pallas_call | solution.py:441

commit v4 on v3

--- a/solution.py
+++ b/solution.py
@@ -33,10 +33,10 @@
     cell, net, grad, w1, w2, slot_cell, net_pin, count, code,
     cell_t, net_t, w1_t, cell_all, net_all, grad_all, hot_all, pre_all, hid_grad_all, pre_grad_all, total,
     send, recv, code_recv, ret_send, ret_recv,
-    core_send, core_recv, part_core, bat_send, bat_recv, part_bat, z_send, z_recv,
+    core_send, core_recv, bat_send, bat_recv, part_bat, z_send, z_recv,
     load_sem,
     send_sem, recv_sem, code_ssem, code_rsem, ret_ssem, ret_rsem,
-    core_sem, bat_ssem, bat_rsem, z_ssem, z_rsem, gcore_sem, gbat_ssem, gbat_rsem, gz_ssem, gz_rsem,
+    core_ssem, core_rsem, bat_ssem, bat_rsem, z_ssem, z_rsem, gcore_ssem, gcore_rsem, gbat_ssem, gbat_rsem, gz_ssem, gz_rsem,
 ):
     bat = lax.axis_index("batch")
     me = lax.axis_index("dom")
@@ -194,12 +194,26 @@
 
     lax.fori_loop(0, depth, late, 0)
 
-    core_send[...] = total[pl.ds(pl.multiple_of((1 - core) * half, half), half), :].astype(BF)
-    core_copy = pltpu.make_async_remote_copy(
-        src_ref=core_send, dst_ref=core_recv, send_sem=core_sem.at[0], recv_sem=core_sem.at[1],
-        device_id=(bat, sibling), device_id_type=MESH,
-    )
-    core_copy.start()
+    rows_b = part_bat.shape[0]
+
+    def own_rows(side, piece):
+        start = pl.multiple_of(side * half + piece * rows_b, rows_b)
+        return total[pl.ds(start, rows_b), :]
+
+    def core_copy(piece):
+        return pltpu.make_async_remote_copy(
+            src_ref=core_send.at[piece], dst_ref=core_recv.at[piece],
+            send_sem=core_ssem.at[piece], recv_sem=core_rsem.at[piece],
+            device_id=(bat, sibling), device_id_type=MESH,
+        )
+
+    def core_go(k, carry):
+        piece = lax.rem(bat + k, batches)
+        core_send[piece] = own_rows(1 - core, piece).astype(BF)
+        core_copy(piece).start()
+        return carry
+
+    lax.fori_loop(1, batches + 1, core_go, 0)
     net_out[...] = jnp.zeros_like(net_out)
 
     def net_side(j, carry):
@@ -208,10 +222,6 @@
         return carry
 
     lax.fori_loop(0, depth, net_side, 0)
-    core_copy.wait()
-    mine = total[pl.ds(pl.multiple_of(core * half, half), half), :] + core_recv[...].astype(F32)
-    part_core[...] = mine.reshape(part_core.shape)
-    bat_send[...] = mine.astype(BF).reshape(bat_send.shape)
 
     def bat_copy(to, frm):
         return pltpu.make_async_remote_copy(
@@ -221,11 +231,15 @@
         )
 
     def bat_go(k, carry):
-        bat_copy(lax.rem(bat + k, batches), bat).start()
+        to = lax.rem(bat + k, batches)
+        core_copy(to).wait_recv()
+        bat_send[to] = (own_rows(core, to) + core_recv[to].astype(F32)).astype(BF)
+        bat_copy(to, bat).start()
         return carry
 
     lax.fori_loop(1, batches, bat_go, 0)
-    part_bat[...] = part_core[bat]
+    core_copy(bat).wait_recv()
+    part_bat[...] = own_rows(core, bat) + core_recv[bat].astype(F32)
 
     def bat_add(k, carry):
         frm = lax.rem(bat - k + batches, batches)
@@ -297,23 +311,22 @@
         gbat_copy(lax.rem(bat + k, batches), bat).start()
         return carry
 
+    def gcore_copy(side, piece):
+        return pltpu.make_async_remote_copy(
+            src_ref=full.at[side, piece], dst_ref=full.at[side, piece],
+            send_sem=gcore_ssem.at[piece], recv_sem=gcore_rsem.at[piece],
+            device_id=(bat, sibling), device_id_type=MESH,
+        )
+
     def gbat_wait(k, carry):
         frm = lax.rem(bat - k + batches, batches)
         gbat_copy(frm, frm).wait_recv()
+        gcore_copy(core, frm).start()
         return carry
 
     lax.fori_loop(1, batches, gbat_go, 0)
-
+    gcore_copy(core, bat).start()
     lax.fori_loop(1, batches, gbat_wait, 0)
-
-    def gcore_copy(frm):
-        return pltpu.make_async_remote_copy(
-            src_ref=full.at[frm], dst_ref=full.at[frm],
-            send_sem=gcore_sem.at[0], recv_sem=gcore_sem.at[1],
-            device_id=(bat, sibling), device_id_type=MESH,
-        )
-
-    gcore_copy(core).start()
 
     cell_out[...] = mm_t(cell_hot(me), ret_send[me])
 
@@ -325,7 +338,11 @@
 
     lax.fori_loop(1, owners, gather_back, 0)
 
-    gcore_copy(1 - core).wait_recv()
+    def gcore_wait(piece, carry):
+        gcore_copy(1 - core, piece).wait_recv()
+        return carry
+
+    lax.fori_loop(0, batches, gcore_wait, 0)
 
     def drain_dom(k, carry):
         to = lax.rem(me + k, owners)
@@ -350,7 +367,13 @@
     lax.fori_loop(1, owners, drain_dom, 0)
     lax.fori_loop(1, batches, drain_batch, 0)
     lax.fori_loop(1, depth, drain_z, 0)
-    gcore_copy(core).wait_send()
+
+    def drain_core(piece, carry):
+        core_copy(piece).wait_send()
+        gcore_copy(core, piece).wait_send()
+        return carry
+
+    lax.fori_loop(0, batches, drain_core, 0)
 
 
 def finish(scale, cell_sum, net_sum, full, cell_out, net_out, first, second):
@@ -420,9 +443,8 @@
             vmem((owners, 8, capacity), jnp.int32),
             vmem((owners, feat, capacity), BF),
             vmem((owners, feat, capacity), BF),
-            vmem((half, width), BF),
-            vmem((half, width), BF),
-            vmem((batches, rows_b, width), F32),
+            vmem((batches, rows_b, width), BF),
+            vmem((batches, rows_b, width), BF),
             vmem((batches, rows_b, width), BF),
             vmem((batches, rows_b, width), BF),
             vmem((rows_b, width), F32),
@@ -431,8 +453,8 @@
             dma((8,)),
             dma((owners,)), dma((owners,)), dma((owners,)), dma((owners,)),
             dma((owners,)), dma((owners,)),
-            dma((2,)), dma((batches,)), dma((batches,)), dma((depth,)), dma((depth,)),
-            dma((2,)), dma((batches,)), dma((batches,)), dma((depth,)), dma((depth,)),
+            dma((batches,)), dma((batches,)), dma((batches,)), dma((batches,)), dma((depth,)), dma((depth,)),
+            dma((batches,)), dma((batches,)), dma((batches,)), dma((batches,)), dma((depth,)), dma((depth,)),
         ],
         compiler_params=pltpu.CompilerParams(
             collective_id=0, has_side_effects=True, vmem_limit_bytes=60 * 1024 * 1024

time: 77.4 us -> 77.1 us (level)
  no operation moved by 1% of the time
where the time goes in v4:
time: 77.1 us; the launch traced here: 76.9 us
  Pallas kernels  76.2 us (99%)
    pallas_call x1, Pallas kernels, on_device(): pl.pallas_call(functools.partial(kernel, batches, owners, rows_z), out_sh...  72.4 us
    pallas_call x1, Pallas kernels, on_device(): pl.pallas_call(functools.partial(finish, scale), out_shape=(jax.ShapeDtyp...  3.85 us

profile of v4, /device:TPU:0, one launch (start us, length us, event | category | flops | bytes accessed | tf_op | source)
XLA Modules:
  0.0 76.9 jit_solution(4591922945980186724)
XLA Ops:
  0.6 72.4 %shard_map.111 = (f32[512,256]{1,0:T(8,128)}, f32[512,256]{1,0:T(8,128)}, bf16[2,4,64,768]{3,2,1,0:T(8,128)(2,1)}) custom-call(bf16[512,256]{1,0:T(8,128)(2,1)} %bitcast.10, bf16[512,256]{1,0:T(8,128)(2,1)} %bitcast.11, bf16[512,256]{1,0:T(8,128)(2,1)} %bitcast.12, bf16[512,512]{1,0:T(8,128)(2,1)} %w1_hbm.1, bf16[512,256]{1,0:T(8,128)(2,1)} %w2_hbm.1, ...), custom_call_target="tpu_custom_call" | custom-call | tf_op jit(solution)/shard_map/pallas_call | solution.py:411
  73.0 3.8 %shard_map.112 = (f32[512,256]{1,0:T(8,128)}, f32[512,256]{1,0:T(8,128)}, f32[512,512]{1,0:T(8,128)}, f32[512,256]{1,0:T(8,128)}) custom-call(f32[512,256]{1,0:T(8,128)} %get-tuple-element.11.cell_sum, f32[512,256]{1,0:T(8,128)} %get-tuple-element.12.net_sum, bf16[512,768]{1,0:T(8,128)(2,1)} %bitcast.9), custom_call_target="tpu_custom_call" | custom-call | tf_op jit(solution)/shard_map/pallas_call | solution.py:463

commit v5 on v4

--- a/solution.py
+++ b/solution.py
@@ -406,7 +406,7 @@
     on_chip = pl.BlockSpec(memory_space=pltpu.VMEM)
 
     def block(rows, columns):
-        return pl.BlockSpec((rows // 4, columns), lambda i: (i, 0))
+        return pl.BlockSpec((rows // 2, columns), lambda i: (i, 0))
 
     cell_sum, net_sum, full = pl.pallas_call(
         functools.partial(kernel, batches, owners, rows_z),
@@ -468,7 +468,7 @@
             jax.ShapeDtypeStruct((fan_in, mid), F32),
             jax.ShapeDtypeStruct((mid, feat), F32),
         ),
-        grid=(4,),
+        grid=(2,),
         in_specs=[block(cells, feat), block(nets, feat), block(fan_in, width)],
         out_specs=[block(cells, feat), block(nets, feat), block(fan_in, mid), block(mid, feat)],
     )(cell_sum, net_sum, full.reshape(fan_in, width))

time: 77.1 us -> 75.9 us (0.984)
  Pallas kernels: 76.2 us -> 75.1 us
    pallas_call x1, Pallas kernels: 3.85 us -> 2.71 us  [on_device(): pl.pallas_call(functools.partial(finish, scale), out_shape=(jax.ShapeDtyp...]
where the time goes in v5:
time: 75.9 us; the launch traced here: 75.7 us
  Pallas kernels  75.1 us (99%)
    pallas_call x1, Pallas kernels, on_device(): pl.pallas_call(functools.partial(kernel, batches, owners, rows_z), out_sh...  72.4 us
    pallas_call x1, Pallas kernels, on_device(): pl.pallas_call(functools.partial(finish, scale), out_shape=(jax.ShapeDtyp...  2.71 us

profile of v5, /device:TPU:0, one launch (start us, length us, event | category | flops | bytes accessed | tf_op | source)
XLA Modules:
  0.0 75.7 jit_solution(12799874266676615351)
XLA Ops:
  0.6 72.4 %shard_map.111 = (f32[512,256]{1,0:T(8,128)}, f32[512,256]{1,0:T(8,128)}, bf16[2,4,64,768]{3,2,1,0:T(8,128)(2,1)}) custom-call(bf16[512,256]{1,0:T(8,128)(2,1)} %bitcast.10, bf16[512,256]{1,0:T(8,128)(2,1)} %bitcast.11, bf16[512,256]{1,0:T(8,128)(2,1)} %bitcast.12, bf16[512,512]{1,0:T(8,128)(2,1)} %w1_hbm.1, bf16[512,256]{1,0:T(8,128)(2,1)} %w2_hbm.1, ...), custom_call_target="tpu_custom_call" | custom-call | tf_op jit(solution)/shard_map/pallas_call | solution.py:411
  73.0 2.7 %shard_map.112 = (f32[512,256]{1,0:T(8,128)}, f32[512,256]{1,0:T(8,128)}, f32[512,512]{1,0:T(8,128)}, f32[512,256]{1,0:T(8,128)}) custom-call(f32[512,256]{1,0:T(8,128)} %get-tuple-element.11.cell_sum, f32[512,256]{1,0:T(8,128)} %get-tuple-element.12.net_sum, bf16[512,768]{1,0:T(8,128)(2,1)} %bitcast.9), custom_call_target="tpu_custom_call" | custom-call | tf_op jit(solution)/shard_map/pallas_call | solution.py:463
